TPU v7x, 32 devices: a whole 2x2x4 slice. The times are simulated.
32 devices in a mesh: grp: 4 (over z), mem: 8 (over y, x, core).
Axes of the slice: x: 2, y: 2, z: 4, core: 2. Of those that a mesh axis runs over, the one named last changes fastest.
Arguments:
- bin_sketch: bfloat16 [256, 1024], P(('grp', 'mem')), may hold values from -6 to 6
- rep_sketch: bfloat16 [8192, 1024], P(('grp', 'mem')), may hold values from -6 to 6
- bin_profile: bfloat16 [256, 32768], P('grp', 'mem'), may hold values from -6 to 6
- member_profile: bfloat16 [12, 256, 32768], P('grp', None, 'mem'), may hold values from -6 to 6
- bin_routes: int32 [256, 2], P('grp'), may hold values from 0 to 11, all different within a row; in each aligned block of 64 rows (0 to 63, 64 to 127, ...) at most 16 rows name the same one
- owner_slot: int32 [12], replicated, may hold values from 0 to 11, each once
- cluster_sizes: int32 [12], replicated, may hold values from 128 to 256, as said below
Outputs:
- coarse_scores: bfloat16 [256, 8192], P(None, ('grp', 'mem'))
- fine_scores: float32 [256, 2, 256], P('grp', None, 'mem')
Inputs may be any that keep to these rules, and one draw needn't show every extreme that they name: `bin_routes`: within the bins of one index of grp (64 consecutive bins), no cluster is named by more than 16 routes, a bound that some block reaches; the two clusters of a bin differ. `owner_slot`: A permutation. `cluster_sizes`: each a multiple of 128.
All inputs are finite; a program needn't handle non-finite values.
Results may differ from a plain program's by a relative error of at most 0.001.
Values may be sent and summed in bfloat16 or wider, within the bound.
No kernel may reach another device: no remote copies, remote signals or barrier semaphores. Data moves between devices by JAX's collectives and lax.ppermute only.
A program may use at most 128 MiB of HBM per device.

v0:
```python
import jax
import jax.numpy as jnp
from jax import lax
from jax.sharding import PartitionSpec as P

FW = 32768
MOST = 16


def local(
    bin_sketch, rep_sketch, bin_profile, member_profile, bin_routes, owner_slot, cluster_sizes
):
    coarse_scale = bin_sketch.shape[1] ** (-0.5)
    group_rows = lax.all_gather(bin_sketch, "mem", axis=0, tiled=True)
    product = lax.dot_general(
        lax.all_gather(group_rows, "grp", axis=0, tiled=True),
        rep_sketch,
        (((1,), (1,)), ((), ())),
        preferred_element_type=jnp.float32,
    )
    coarse_scores = (product * coarse_scale).astype(jnp.bfloat16)
    rows_here, width_here = bin_profile.shape
    slot_count, members, _ = member_profile.shape
    groups = lax.axis_size("grp")
    cluster_total = owner_slot.shape[0]
    capacity = groups * slot_count * MOST
    route_flat = bin_routes.reshape(-1)
    cluster_ids = jnp.arange(cluster_total, dtype=jnp.int32)
    route_hit = (route_flat[:, None] == cluster_ids[None, :]).astype(jnp.int32)
    storage = jnp.sum(route_hit * owner_slot[None, :], axis=1)
    route_size = jnp.sum(route_hit * cluster_sizes[None, :], axis=1)
    route_rank = jnp.sum((jnp.cumsum(route_hit, axis=0) - route_hit) * route_hit, axis=1)
    slot_index = storage * MOST + route_rank
    source = bin_profile[jnp.arange(route_flat.shape[0], dtype=jnp.int32) // 2]
    outgoing = jnp.zeros((capacity, width_here), jnp.bfloat16).at[slot_index].set(source)
    outgoing = outgoing.reshape(groups, slot_count * MOST, width_here)
    incoming = lax.all_to_all(outgoing, "grp", split_axis=0, concat_axis=0, tiled=True)
    incoming = incoming.reshape(groups, slot_count, MOST, width_here)
    partial_value = jnp.einsum(
        "gsmc,sjc->gsmj", incoming, member_profile, preferred_element_type=jnp.float32
    )
    summed = lax.psum_scatter(partial_value, "mem", scatter_dimension=3, tiled=True)
    returned = lax.all_to_all(summed, "grp", split_axis=0, concat_axis=0, tiled=True)
    member_local = returned.shape[3]
    route_scores = returned.reshape(capacity, member_local)[slot_index] * FW ** (-0.5)
    column = lax.axis_index("mem") * member_local + jnp.arange(member_local, dtype=jnp.int32)
    member_live = column[None, :] < route_size[:, None]
    fine_scores = jnp.where(member_live, route_scores, 0.0).reshape(rows_here, 2, member_local)
    return (coarse_scores, fine_scores)


def solution(mesh):
    return jax.shard_map(
        local,
        mesh=mesh,
        in_specs=(
            P(("grp", "mem"), None),
            P(("grp", "mem"), None),
            P("grp", "mem"),
            P("grp", None, "mem"),
            P("grp", None),
            P(),
            P(),
        ),
        out_specs=(P(None, ("grp", "mem")), P("grp", None, "mem")),
        check_vma=False,
    )
```

profile of v0, /device:TPU:0, one launch (start us, length us, event | category | flops | bytes accessed | tf_op | source)
XLA Modules:
  0.0 133.0 jit_solution(8496143700417119367)
XLA Ops:
  7.2 0.0 copy-start
  7.2 0.8 copy.17
  8.0 0.1 eq.15
  8.2 0.1 fusion.12
  8.3 0.2 reduce_window_sum.11
  8.4 0.9 select_reduce_fusion.2
  9.3 0.0 copy-done
  9.3 6.4 %scatter_custom_fusion = bf16[192,4096]{1,0:T(8,128)(2,1)} fusion(s32[128]{0:T(128)S(1)} %fusion.14, bf16[64,4096]{1,0:T(8,128)(2,1)S(1)} %copy-done, s32[1024]{0:T(1024)S(1)} %pad_clamp_fusion.1, bf16[]{:T(256)} %constant.36.clone.1), kind=kCustom, calls=%fused_computation.9 | custom fusion | bytes 1572866 | tf_op jit(solution)/shard_map/scatter | solution.py:35
  15.7 0.0 copy-start.2
  15.7 6.5 %all-to-all-start = ((bf16[4,48,4096]{2,1,0:T(8,128)(2,1)}), bf16[4,48,4096]{2,1,0:T(8,128)(2,1)S(1)}, u32[]{:S(2)}, u32[]{:S(2)}) async-start(bf16[4,48,4096]{2,1,0:T(8,128)(2,1)} %bitcast.3), calls=%async_computation | async-start | bytes 3145728 | tf_op jit(solution)/shard_map/all_to_all | solution.py:37
  22.2 0.0 reduce-scatter.4.cloned.1.call-start
  22.2 0.0 copy-done.2
  22.2 9.2 %all_gather.6 = bf16[64,1024]{1,0:T(8,128)(2,1)S(1)} all-gather(bf16[8,1024]{1,0:T(8,128)(2,1)S(1)} %copy-done.2), channel_id=1, replica_groups=mesh['grp'=4,'mem'=8] {'mem'}, dimensions={0}, use_global_device_ids=true | all-gather | bytes 147456 | tf_op jit(solution)/shard_map/all_gather | solution.py:14
  31.4 38.1 %all_gather.7 = bf16[256,1024]{1,0:T(8,128)(2,1)S(1)} all-gather(bf16[64,1024]{1,0:T(8,128)(2,1)S(1)} %all_gather.6), channel_id=1, replica_groups=mesh['grp'=4,'mem'=8] {'grp'}, dimensions={0}, use_global_device_ids=true | all-gather | bytes 655360 | tf_op jit(solution)/shard_map/all_gather | solution.py:16
  69.5 0.0 all-to-all-done
  69.5 4.8 %fusion.4 = f32[4,3,16,256]{3,2,0,1:T(8,128)S(1)} fusion(bf16[3,256,4096]{2,1,0:T(8,128)(2,1)} %param.10, bf16[4,3,16,4096]{3,2,1,0:T(8,128)(2,1)S(1)} %bitcast.25), kind=kOutput, calls=%fused_computation.8 | convolution fusion | flops 402653184 | bytes 8060928 | tf_op jit(solution)/shard_map/gsmc,sjc->gsmj/dot_general | solution.py:39
  74.4 0.0 copy-start.1
  74.4 0.7 copy.23
  75.1 1.5 %reshape.132 = f32[256,192]{1,0:T(8,128)} reshape(f32[256,3,4,16]{3,2,1,0:T(4,128)S(1)} %bitcast.24) | data formatting | bytes 393216
  76.6 0.0 reduce-scatter.4.cloned.1.call-update
  76.6 0.0 copy-done.1
  76.6 1.0 fusion.3
  77.6 33.7 %reduce-scatter.4.cloned.1.call-done = f32[32,192]{1,0:T(8,128)} async-done(((f32[256,192]{1,0:T(8,128)}), f32[32,192]{1,0:T(8,128)}) %reduce-scatter.4.cloned.1.call-update) | async-done | bytes 24592
  111.4 0.9 reshape.133
  112.3 0.1 copy.20
  112.4 0.7 reshape.140
  113.1 4.6 %all-to-all-start.1 = ((f32[4,1,1536]{2,1,0:T(1,128)}), f32[4,1,1536]{2,1,0:T(1,128)S(1)}, u32[]{:S(2)}, u32[]{:S(2)}) async-start(f32[4,1,1536]{2,1,0:T(1,128)} %reshape.140), calls=%async_computation.1 | async-start | bytes 49152 | tf_op jit(solution)/shard_map/all_to_all | solution.py:43
  117.7 0.1 lt.38
  117.9 0.1 copy.18
  117.9 5.4 %all-to-all-done.1 = f32[4,1,1536]{2,1,0:T(1,128)S(1)} async-done(((f32[4,1,1536]{2,1,0:T(1,128)}), f32[4,1,1536]{2,1,0:T(1,128)S(1)}, u32[]{:S(2)}, u32[]{:S(2)}) %all-to-all-start.1) | async-done | bytes 24608 | tf_op jit(solution)/shard_map/all_to_all | solution.py:43
  123.4 0.5 broadcast.125
  123.9 0.7 reduce
  124.6 0.1 reshape.141
  124.7 0.6 gather_fusion
  125.3 0.1 copy.21
  125.4 0.7 compare_select_fusion
  (6 shorter events, 0.0 us)
Async XLA Ops:
  7.2 2.2 %copy-start = (bf16[64,4096]{1,0:T(8,128)(2,1)S(1)}, bf16[64,4096]{1,0:T(8,128)(2,1)}, u32[]{:S(2)}) copy-start(bf16[64,4096]{1,0:T(8,128)(2,1)} %param.9) | copy-start | bytes 1572868
  15.7 6.5 %copy-start.2 = (bf16[8,1024]{1,0:T(8,128)(2,1)S(1)}, bf16[8,1024]{1,0:T(8,128)(2,1)}, u32[]{:S(2)}) copy-start(bf16[8,1024]{1,0:T(8,128)(2,1)} %param.7) | copy-start | bytes 49156
  15.7 53.8 %all-to-all-start = ((bf16[4,48,4096]{2,1,0:T(8,128)(2,1)}), bf16[4,48,4096]{2,1,0:T(8,128)(2,1)S(1)}, u32[]{:S(2)}, u32[]{:S(2)}) async-start(bf16[4,48,4096]{2,1,0:T(8,128)(2,1)} %bitcast.3), calls=%async_computation | async-start | bytes 3145728 | tf_op jit(solution)/shard_map/all_to_all | solution.py:37
  22.2 89.2 %reduce-scatter.4.cloned.1.call-start = ((), (), s32[]{:S(2)}) async-start(), calls=%async_computation.3 | async-start | bytes 294912
  74.4 2.3 %copy-start.1 = (bf16[256,1024]{1,0:T(8,128)(2,1)S(1)}, bf16[256,1024]{1,0:T(8,128)(2,1)}, u32[]{:S(2)}) copy-start(bf16[256,1024]{1,0:T(8,128)(2,1)} %param.8) | copy-start | bytes 1572868
  113.1 10.2 %all-to-all-start.1 = ((f32[4,1,1536]{2,1,0:T(1,128)}), f32[4,1,1536]{2,1,0:T(1,128)S(1)}, u32[]{:S(2)}, u32[]{:S(2)}) async-start(f32[4,1,1536]{2,1,0:T(1,128)} %reshape.140), calls=%async_computation.1 | async-start | bytes 49152 | tf_op jit(solution)/shard_map/all_to_all | solution.py:43
Sparse Core Ops, SparseCore 0:
  76.7 34.6 reduce-scatter.3
where the time goes:
time: 133 us
  blocking collectives  47.3 us (36%)
  waiting for transfers between devices  39.2 us (29%)
  between operations  14.1 us (11%)
  local copies, waits for them, and re-layouts  12.8 us (10%)
  starting transfers between devices  11.1 us (8%)
  matrix products  5.81 us (4%)
  other arithmetic  2.59 us (2%)
    all_gather x1, blocking collectives, local(): lax.all_gather(group_rows, 'grp', axis=0, tiled=True)  38.1 us
    unnamed x2, waiting for transfers between devices  33.8 us
    all_gather x1, blocking collectives, local(): group_rows = lax.all_gather(bin_sketch, 'mem', axis=0, tiled=True)  9.22 us
    all_to_all x1, starting transfers between devices, local(): lax.all_to_all(outgoing, 'grp', split_axis=0, concat_axis=0, tiled=True)  6.48 us
    scatter x1, local copies, waits for them, and re-layouts, local(): jnp.zeros((capacity, width_here), jnp.bfloat16).at[slot_index].set(source)  6.38 us
    all_to_all x1, waiting for transfers between devices, local(): lax.all_to_all(summed, 'grp', split_axis=0, concat_axis=0, tiled=True)  5.43 us
    dot_general x1, matrix products, local(): jnp.einsum('gsmc,sjc->gsmj', incoming, member_profile, preferred_element_...  4.81 us
    unnamed x12, local copies, waits for them, and re-layouts  4.76 us
  transfers between devices with their start and end apart: 3, of which 2 were waited for; matrix products, arithmetic and copies ran while one was open for 1% of the time, Pallas kernels for 0%

commit v1 on v0

--- a/solution.py
+++ b/solution.py
@@ -40,7 +40,19 @@
         "gsmc,sjc->gsmj", incoming, member_profile, preferred_element_type=jnp.float32
     )
     summed = lax.psum_scatter(partial_value, "mem", scatter_dimension=3, tiled=True)
-    returned = lax.all_to_all(summed, "grp", split_axis=0, concat_axis=0, tiled=True)
+    ways, here = (lax.axis_size("grp"), lax.axis_index("grp"))
+    width = summed.shape[0] // ways
+    shape = list(summed.shape)
+    shape[0] = width
+    height = shape[0]
+    shape[0] = height * ways
+    full = jnp.zeros(shape, summed.dtype)
+    for mask in range(ways):
+        part = lax.dynamic_slice_in_dim(summed, (here ^ mask) * width, width, axis=0)
+        if mask:
+            part = lax.ppermute(part, "grp", [(d, d ^ mask) for d in range(ways)])
+        full = lax.dynamic_update_slice_in_dim(full, part, (here ^ mask) * height, axis=0)
+    returned = full
     member_local = returned.shape[3]
     route_scores = returned.reshape(capacity, member_local)[slot_index] * FW ** (-0.5)
     column = lax.axis_index("mem") * member_local + jnp.arange(member_local, dtype=jnp.int32)

time: 133 us -> 131 us (0.985)
    all_to_all x1 -> x0, waiting for transfers between devices: 5.43 us -> none  [local(): lax.all_to_all(summed, 'grp', split_axis=0, concat_axis=0, tiled=True)]
    ppermute x0 -> x3, waiting for transfers between devices: none -> 5.08 us  [local(): part = lax.ppermute(part, 'grp', [(d, d ^ mask) for d in range(ways)])]
    all_to_all x1 -> x0, starting transfers between devices: 4.6 us -> none  [local(): lax.all_to_all(summed, 'grp', split_axis=0, concat_axis=0, tiled=True)]
    ppermute x0 -> x3, starting transfers between devices: none -> 4.42 us  [local(): part = lax.ppermute(part, 'grp', [(d, d ^ mask) for d in range(ways)])]
    unnamed x12 -> x14, local copies, waits for them, and re-layouts: 4.76 us -> 4.26 us
  transfers between devices with their start and end apart: 3 -> 5, of which waited for: 2 -> 3; matrix products, arithmetic and copies ran while one was open for 1% -> 1% of each run, Pallas kernels for 0% -> 0%
where the time goes in v1:
time: 131 us
  blocking collectives  47.3 us (36%)
  waiting for transfers between devices  38.6 us (29%)
  between operations  14.2 us (11%)
  local copies, waits for them, and re-layouts  11.9 us (9%)
  starting transfers between devices  10.9 us (8%)
  matrix products  5.83 us (4%)
  other arithmetic  1.88 us (1%)
    all_gather x1, blocking collectives, local(): lax.all_gather(group_rows, 'grp', axis=0, tiled=True)  38.1 us
    unnamed x2, waiting for transfers between devices  33.5 us
    all_gather x1, blocking collectives, local(): group_rows = lax.all_gather(bin_sketch, 'mem', axis=0, tiled=True)  9.22 us
    all_to_all x1, starting transfers between devices, local(): lax.all_to_all(outgoing, 'grp', split_axis=0, concat_axis=0, tiled=True)  6.48 us
    scatter x1, local copies, waits for them, and re-layouts, local(): jnp.zeros((capacity, width_here), jnp.bfloat16).at[slot_index].set(source)  6.38 us
    ppermute x3, waiting for transfers between devices, local(): part = lax.ppermute(part, 'grp', [(d, d ^ mask) for d in range(ways)])  5.08 us
    dot_general x1, matrix products, local(): jnp.einsum('gsmc,sjc->gsmj', incoming, member_profile, preferred_element_...  4.81 us
    ppermute x3, starting transfers between devices, local(): part = lax.ppermute(part, 'grp', [(d, d ^ mask) for d in range(ways)])  4.42 us
  transfers between devices with their start and end apart: 5, of which 3 were waited for; matrix products, arithmetic and copies ran while one was open for 1% of the time, Pallas kernels for 0%

profile of v1, /device:TPU:0, one launch (start us, length us, event | category | flops | bytes accessed | tf_op | source)
XLA Modules:
  0.0 130.6 jit_solution(6148901632472915457)
XLA Ops:
  7.2 0.0 copy-start
  7.2 0.8 copy.20
  8.0 0.1 eq.15
  8.1 0.1 fusion.12
  8.2 0.2 reduce_window_sum.11
  8.4 0.9 select_reduce_fusion.2
  9.3 0.0 copy-done
  9.3 6.4 %scatter_custom_fusion = bf16[192,4096]{1,0:T(8,128)(2,1)} fusion(s32[128]{0:T(128)S(1)} %get-tuple-element.10, bf16[64,4096]{1,0:T(8,128)(2,1)S(1)} %copy-done, s32[1024]{0:T(1024)S(1)} %pad_clamp_fusion.1, bf16[]{:T(256)} %constant.44.clone.1), kind=kCustom, calls=%fused_computation.9 | custom fusion | bytes 1572866 | tf_op jit(solution)/shard_map/scatter | solution.py:35
  15.7 0.0 copy-start.2
  15.7 6.5 %all-to-all-start = ((bf16[4,48,4096]{2,1,0:T(8,128)(2,1)}), bf16[4,48,4096]{2,1,0:T(8,128)(2,1)S(1)}, u32[]{:S(2)}, u32[]{:S(2)}) async-start(bf16[4,48,4096]{2,1,0:T(8,128)(2,1)} %bitcast.3), calls=%async_computation | async-start | bytes 3145728 | tf_op jit(solution)/shard_map/all_to_all | solution.py:37
  22.2 0.0 reduce-scatter.4.cloned.1.call-start
  22.2 0.0 copy-done.2
  22.2 9.2 %all_gather.6 = bf16[64,1024]{1,0:T(8,128)(2,1)S(1)} all-gather(bf16[8,1024]{1,0:T(8,128)(2,1)S(1)} %copy-done.2), channel_id=1, replica_groups=mesh['grp'=4,'mem'=8] {'mem'}, dimensions={0}, use_global_device_ids=true | all-gather | bytes 147456 | tf_op jit(solution)/shard_map/all_gather | solution.py:14
  31.4 38.1 %all_gather.7 = bf16[256,1024]{1,0:T(8,128)(2,1)S(1)} all-gather(bf16[64,1024]{1,0:T(8,128)(2,1)S(1)} %all_gather.6), channel_id=1, replica_groups=mesh['grp'=4,'mem'=8] {'grp'}, dimensions={0}, use_global_device_ids=true | all-gather | bytes 655360 | tf_op jit(solution)/shard_map/all_gather | solution.py:16
  69.5 0.0 all-to-all-done
  69.5 4.8 %fusion.4 = f32[4,3,16,256]{3,2,0,1:T(8,128)S(1)} fusion(bf16[3,256,4096]{2,1,0:T(8,128)(2,1)} %param.10, bf16[4,3,16,4096]{3,2,1,0:T(8,128)(2,1)S(1)} %bitcast.33), kind=kOutput, calls=%fused_computation.8 | convolution fusion | flops 402653184 | bytes 8060928 | tf_op jit(solution)/shard_map/gsmc,sjc->gsmj/dot_general | solution.py:39
  74.3 0.0 copy-start.1
  74.4 0.7 copy.29
  75.1 1.5 %reshape.132 = f32[256,192]{1,0:T(8,128)} reshape(f32[256,3,4,16]{3,2,1,0:T(4,128)S(1)} %bitcast.32) | data formatting | bytes 393216
  76.6 0.0 reduce-scatter.4.cloned.1.call-update
  76.6 0.1 lt.54
  76.8 0.1 copy.21
  76.8 0.0 copy-done.1
  76.8 1.0 fusion.3
  77.8 33.5 %reduce-scatter.4.cloned.1.call-done = f32[32,192]{1,0:T(8,128)} async-done(((f32[256,192]{1,0:T(8,128)}), f32[32,192]{1,0:T(8,128)}) %reduce-scatter.4.cloned.1.call-update) | async-done | bytes 24592
  111.4 0.9 reshape.133
  112.3 0.2 constant_dynamic-slice_fusion
  112.5 0.1 copy.31
  112.5 0.1 copy.32
  112.6 1.5 %collective-permute-start = (f32[1,3,16,32]{3,2,0,1:T(8,128)S(1)}, f32[1,3,16,32]{3,2,0,1:T(8,128)S(1)}, u32[]{:S(2)}, u32[]{:S(2)}) collective-permute-start(f32[1,3,16,32]{3,2,0,1:T(8,128)S(1)} %copy.32), channel_id=1, source_target_pairs={{0,8},{8,0},{16,24},{24,16},{1,9},{9,1},{17,25},{25,17},{2,10},{10... | collective-permute-start | bytes 18440 | tf_op jit(solution)/shard_map/ppermute | solution.py:53
  114.1 0.1 copy.33
  114.2 2.4 %collective-permute-start.1 = (f32[1,3,16,32]{3,2,0,1:T(8,128)S(1)}, f32[1,3,16,32]{3,2,0,1:T(8,128)S(1)}, u32[]{:S(2)}, u32[]{:S(2)}) collective-permute-start(f32[1,3,16,32]{3,2,0,1:T(8,128)S(1)} %copy.33), channel_id=1, source_target_pairs={{0,16},{8,24},{16,0},{24,8},{1,17},{9,25},{17,1},{25,9},{2,18},{10... | collective-permute-start | bytes 18440 | tf_op jit(solution)/shard_map/ppermute | solution.py:53
  116.6 0.1 copy.34
  116.7 0.5 collective-permute-start.2
  117.2 0.0 collective-permute-done
  117.2 1.9 %collective-permute-done.1 = f32[1,3,16,32]{3,2,0,1:T(8,128)S(1)} collective-permute-done((f32[1,3,16,32]{3,2,0,1:T(8,128)S(1)}, f32[1,3,16,32]{3,2,0,1:T(8,128)S(1)}, u32[]{:S(2)}, u32[]{:S(2)}) %collective-permute-start.1) | collective-permute-done | bytes 6176 | tf_op jit(solution)/shard_map/ppermute | solution.py:53
  119.2 3.1 %collective-permute-done.2 = f32[1,3,16,32]{3,2,0,1:T(8,128)S(1)} collective-permute-done((f32[1,3,16,32]{3,2,0,1:T(8,128)S(1)}, f32[1,3,16,32]{3,2,0,1:T(8,128)S(1)}, u32[]{:S(2)}, u32[]{:S(2)}) %collective-permute-start.2) | collective-permute-done | bytes 6176 | tf_op jit(solution)/shard_map/ppermute | solution.py:53
  122.3 0.6 gather_fusion
  123.0 0.1 copy.27
  123.1 0.7 compare_select_fusion
  (10 shorter events, 0.1 us)
Async XLA Ops:
  7.2 2.2 %copy-start = (bf16[64,4096]{1,0:T(8,128)(2,1)S(1)}, bf16[64,4096]{1,0:T(8,128)(2,1)}, u32[]{:S(2)}) copy-start(bf16[64,4096]{1,0:T(8,128)(2,1)} %param.9) | copy-start | bytes 1572868
  15.7 6.5 %copy-start.2 = (bf16[8,1024]{1,0:T(8,128)(2,1)S(1)}, bf16[8,1024]{1,0:T(8,128)(2,1)}, u32[]{:S(2)}) copy-start(bf16[8,1024]{1,0:T(8,128)(2,1)} %param.7) | copy-start | bytes 49156
  15.7 53.8 %all-to-all-start = ((bf16[4,48,4096]{2,1,0:T(8,128)(2,1)}), bf16[4,48,4096]{2,1,0:T(8,128)(2,1)S(1)}, u32[]{:S(2)}, u32[]{:S(2)}) async-start(bf16[4,48,4096]{2,1,0:T(8,128)(2,1)} %bitcast.3), calls=%async_computation | async-start | bytes 3145728 | tf_op jit(solution)/shard_map/all_to_all | solution.py:37
  22.2 89.2 %reduce-scatter.4.cloned.1.call-start = ((), (), s32[]{:S(2)}) async-start(), calls=%async_computation.2 | async-start | bytes 294912
  74.3 2.5 %copy-start.1 = (bf16[256,1024]{1,0:T(8,128)(2,1)S(1)}, bf16[256,1024]{1,0:T(8,128)(2,1)}, u32[]{:S(2)}) copy-start(bf16[256,1024]{1,0:T(8,128)(2,1)} %param.8) | copy-start | bytes 1572868
  112.6 4.6 %collective-permute-start = (f32[1,3,16,32]{3,2,0,1:T(8,128)S(1)}, f32[1,3,16,32]{3,2,0,1:T(8,128)S(1)}, u32[]{:S(2)}, u32[]{:S(2)}) collective-permute-start(f32[1,3,16,32]{3,2,0,1:T(8,128)S(1)} %copy.32), channel_id=1, source_target_pairs={{0,8},{8,0},{16,24},{24,16},{1,9},{9,1},{17,25},{25,17},{2,10},{10... | collective-permute-start | bytes 18440 | tf_op jit(solution)/shard_map/ppermute | solution.py:53
  114.2 5.0 %collective-permute-start.1 = (f32[1,3,16,32]{3,2,0,1:T(8,128)S(1)}, f32[1,3,16,32]{3,2,0,1:T(8,128)S(1)}, u32[]{:S(2)}, u32[]{:S(2)}) collective-permute-start(f32[1,3,16,32]{3,2,0,1:T(8,128)S(1)} %copy.33), channel_id=1, source_target_pairs={{0,16},{8,24},{16,0},{24,8},{1,17},{9,25},{17,1},{25,9},{2,18},{10... | collective-permute-start | bytes 18440 | tf_op jit(solution)/shard_map/ppermute | solution.py:53
  116.7 5.6 %collective-permute-start.2 = (f32[1,3,16,32]{3,2,0,1:T(8,128)S(1)}, f32[1,3,16,32]{3,2,0,1:T(8,128)S(1)}, u32[]{:S(2)}, u32[]{:S(2)}) collective-permute-start(f32[1,3,16,32]{3,2,0,1:T(8,128)S(1)} %copy.34), channel_id=1, source_target_pairs={{0,24},{8,16},{16,8},{24,0},{1,25},{9,17},{17,9},{25,1},{2,26},{10... | collective-permute-start | bytes 18440 | tf_op jit(solution)/shard_map/ppermute | solution.py:53
Sparse Core Ops, SparseCore 0:
  76.7 34.6 reduce-scatter.3
